TPU v7x, 128 devices: a whole 4x4x4 slice. The times are simulated.
128 devices in a mesh: row: 4 (over y_lo, core), col: 32 (over x, z, y_hi).
Axes of the slice: x: 4, y: 4 (y_hi: 2, y_lo: 2; y = y_hi * 2 + y_lo), z: 4, core: 2. Of those that a mesh axis runs over, the one named last changes fastest.
Arguments:
- features: bfloat16 [65536, 256], P(('row', 'col')), may hold values from -6 to 6
- tile_values: bfloat16 [256, 64, 256, 256], P('col', 'row'), may hold values from 0 to 1, as said below
- tile_cols: int32 [256, 64], P('col', 'row'), may hold values from 0 to 63
- tile_counts: int32 [256, 4], P('col', 'row'), may hold values from 1 to 16, as said below
- weight: bfloat16 [256, 256], replicated, may hold values from -0.375 to 0.375
- bias: float32 [256], replicated, may hold values from -3 to 3
- cotangent: bfloat16 [65536, 256], P(('col', 'row')), may hold values from -6 to 6
Outputs:
- layer_out: bfloat16 [65536, 256], P(('col', 'row'))
- feature_grad: bfloat16 [65536, 256], P(('row', 'col'))
- weight_grad: float32 [256, 256], replicated
- bias_grad: float32 [256], replicated
Inputs may be any that keep to these rules, and one draw needn't show every extreme that they name: `tile_values`: nonnegative edge weights. `tile_counts`: every draw has some entry equal to 16; the loads differ between the devices' blocks.
All inputs are finite; a program needn't handle non-finite values.
Results may differ from a plain program's by a relative error of at most 0.025.
Values may be sent and summed in bfloat16 or wider, within the bound.
A program may use at most 128 MiB of HBM per device.

v0:
```python
import math
import jax
import jax.numpy as jnp
from jax import lax
from jax.sharding import PartitionSpec as P


def dense_part(hidden, weight, bias, cotangent):
    preact = jnp.dot(hidden, weight, preferred_element_type=jnp.float32) + bias
    output = jax.nn.silu(preact).astype(jnp.bfloat16)
    sigmoid_value = jax.nn.sigmoid(preact)
    slope = sigmoid_value * (1.0 + preact * (1.0 - sigmoid_value))
    preact_grad = (cotangent.astype(jnp.float32) * slope).astype(jnp.bfloat16)
    weight_grad = lax.dot_general(
        hidden, preact_grad, (((0,), (0,)), ((), ())), preferred_element_type=jnp.float32
    )
    bias_grad = jnp.sum(preact_grad.astype(jnp.float32), axis=0)
    hidden_grad = lax.dot_general(
        preact_grad, weight, (((1,), (1,)), ((), ())), preferred_element_type=jnp.float32
    ).astype(jnp.bfloat16)
    return (output, weight_grad, bias_grad, hidden_grad)


def per_device(features, tile_values, tile_cols, tile_counts, weight, bias, cotangent):
    node_dev, width = features.shape
    row_tiles, slot_count, tile_size, _ = tile_values.shape
    column_block = lax.all_gather(features, "col", axis=0, tiled=True)
    column_tiles = column_block.shape[0] // tile_size
    x_tiles = column_block.reshape(column_tiles, tile_size, width)
    live_counts = tile_counts[:, 0]
    slot_top = jnp.max(live_counts)

    def slot_data(slot):
        values = lax.dynamic_index_in_dim(tile_values, slot, 1, keepdims=False)
        columns = lax.dynamic_index_in_dim(tile_cols, slot, 1, keepdims=False)
        live = slot < live_counts
        return (values, columns, live)

    def forward_slot(slot, running):
        values, columns, live = slot_data(slot)
        picked = jnp.take(x_tiles, columns, axis=0) * live[:, None, None].astype(jnp.bfloat16)
        return running + jnp.einsum(
            "tij,tjf->tif", values, picked, preferred_element_type=jnp.float32
        )

    partial_value = lax.fori_loop(
        0, slot_top, forward_slot, jnp.zeros((row_tiles, tile_size, width), jnp.float32)
    )
    partial_value = partial_value.reshape(row_tiles * tile_size, width)
    node_total = node_dev * lax.axis_size("row") * lax.axis_size("col")
    grad_scale = 1.0 / math.sqrt(node_total)
    own_rows = lax.psum_scatter(
        partial_value.astype(jnp.bfloat16), "row", scatter_dimension=0, tiled=True
    )
    layer_out, weight_grad, bias_grad, hidden_grad = dense_part(own_rows, weight, bias, cotangent)
    weight_grad, bias_grad = lax.psum((weight_grad, bias_grad), ("row", "col"))
    grad_block = lax.all_gather(hidden_grad, "row", axis=0, tiled=True)
    grad_tiles = grad_block.reshape(row_tiles, tile_size, width)

    def backward_slot(slot, running):
        values, columns, live = slot_data(slot)
        contrib = jnp.einsum("tij,tif->tjf", values, grad_tiles, preferred_element_type=jnp.float32)
        contrib = contrib * live[:, None, None].astype(jnp.float32)
        return running.at[columns].add(contrib)

    summed = lax.fori_loop(
        0, slot_top, backward_slot, jnp.zeros((column_tiles, tile_size, width), jnp.float32)
    )
    summed = summed.reshape(column_tiles * tile_size, width)
    feature_grad = lax.psum_scatter(
        summed.astype(jnp.bfloat16), "col", scatter_dimension=0, tiled=True
    )
    return (layer_out, feature_grad, weight_grad * grad_scale, bias_grad * grad_scale)


def solution(mesh):
    placed = (
        P(("row", "col"), None),
        P("col", "row", None, None),
        P("col", "row"),
        P("col", "row"),
        P(),
        P(),
        P(("col", "row"), None),
    )
    return jax.shard_map(
        per_device,
        mesh=mesh,
        in_specs=placed,
        out_specs=(P(("col", "row"), None), P(("row", "col"), None), P(), P()),
        check_vma=False,
    )
```

profile of v0, /device:TPU:0, one launch (start us, length us, event | category | flops | bytes accessed | tf_op | source)
XLA Modules:
  0.0 641.1 jit_solution(3709168496130646856)
XLA Ops:
  8.0 0.8 copy.12
  8.7 1.3 reduce_max.9
  10.0 107.7 %all-gather.3.cloned.1.call-done = bf16[16384,256]{1,0:T(8,128)(2,1)} async-done(((bf16[512,256]{1,0:T(8,128)(2,1)}), bf16[16384,256]{1,0:T(8,128)(2,1)}) %all-gather.3.cloned.1.call-update) | async-done | bytes 8388624 | tf_op jit(solution)/shard_map/all_gather | solution.py:27
  118.0 60.5 %while.20 = (s32[]{:T(128)}, f32[8,256,256]{2,1,0:T(8,128)S(1)}, s32[]{:T(128)}, bf16[8,16,256,256]{3,2,1,0:T(8,128)(2,1)}, s32[8,16]{0,1:T(8,128)S(1)}, /*index...) while((s32[]{:T(128)}, f32[8,256,256]{2,1,0:T(8,128)S(1)}, s32[]{:T(128)}, ...), condition=%wide.region_2.3_spmd, body=%wide.region_1.2_spmd.sunk | while | flops 270009408 | bytes 8393067 | solution.py:46
  119.3 4.0 gather_fusion
  123.3 2.1 convolution_add_fusion.3
  126.8 4.0 gather_fusion
  130.8 2.1 convolution_add_fusion.3
  134.3 4.0 gather_fusion
  138.3 2.1 convolution_add_fusion.3
  141.7 4.0 gather_fusion
  145.8 2.1 convolution_add_fusion.3
  149.2 4.0 gather_fusion
  153.2 2.1 convolution_add_fusion.3
  156.7 4.0 gather_fusion
  160.7 2.1 convolution_add_fusion.3
  164.2 4.0 gather_fusion
  168.2 2.1 convolution_add_fusion.3
  171.7 4.0 gather_fusion
  175.7 2.1 convolution_add_fusion.3
  178.4 1.1 convert_element_type.43
  179.6 76.7 %reduce-scatter.3.cloned.1.call-done = bf16[512,256]{1,0:T(8,128)(2,1)} async-done(((bf16[2048,256]{1,0:T(8,128)(2,1)}), bf16[512,256]{1,0:T(8,128)(2,1)}) %reduce-scatter.3.cloned.1.call-update) | async-done | bytes 262160 | tf_op jit(solution)/shard_map/reduce_scatter | solution.py:52
  256.3 2.1 convert_reduce_fusion
  258.4 1.0 convolution_convert_fusion
  259.4 1.9 fusion.13
  261.4 20.0 %all-gather.5.cloned.1.call-done = bf16[2048,256]{1,0:T(8,128)(2,1)} async-done(((bf16[512,256]{1,0:T(8,128)(2,1)}), bf16[2048,256]{1,0:T(8,128)(2,1)}) %all-gather.5.cloned.1.call-update) | async-done | bytes 1048592 | tf_op jit(solution)/shard_map/all_gather | solution.py:57
  281.4 7.8 %broadcast_in_dim.21 = f32[64,256,256]{2,1,0:T(8,128)} broadcast(f32[]{:T(128)} %constant.49.clone.1), dimensions={} | broadcast | bytes 16777220 | tf_op jit(solution)/shard_map/broadcast_in_dim | solution.py:67
  289.2 55.6 %while.21 = (s32[]{:T(128)}, f32[64,256,256]{2,1,0:T(8,128)}, s32[]{:T(128)}, s32[8,16]{0,1:T(8,128)S(1)}, bf16[8,16,256,256]{3,2,1,0:T(8,128)(2,1)}, /*index=5*...) while((s32[]{:T(128)}, f32[64,256,256]{2,1,0:T(8,128)}, s32[]{:T(128)}, ...), condition=%wide.region_6.7_spmd, body=%wide.region_4.6_spmd.sunk | while | flops 269484064 | bytes 10486107 | solution.py:66
  289.9 1.8 convolution_multiply_fusion.2
  291.7 4.3 scatter_fusion
  296.7 1.8 convolution_multiply_fusion.2
  298.5 4.4 scatter_fusion
  303.6 1.8 convolution_multiply_fusion.2
  305.4 4.2 scatter_fusion
  310.3 1.8 convolution_multiply_fusion.2
  312.1 4.4 scatter_fusion
  317.2 1.8 convolution_multiply_fusion.2
  319.0 4.5 scatter_fusion
  324.2 1.8 convolution_multiply_fusion.2
  326.0 4.4 scatter_fusion
  331.1 1.8 convolution_multiply_fusion.2
  332.9 4.4 scatter_fusion
  338.0 1.8 convolution_multiply_fusion.2
  339.8 4.3 scatter_fusion
  344.8 9.0 %convert_element_type.49 = bf16[64,256,256]{2,1,0:T(8,128)(2,1)} convert(f32[64,256,256]{2,1,0:T(8,128)} %get-tuple-element.81) | non-fusion elementwise | flops 4194304 | bytes 25165824 | tf_op jit(solution)/shard_map/convert_element_type | solution.py:71
  353.8 162.3 %psum.15 = f32[256]{0:T(256)S(1)} all-reduce(f32[256]{0:T(256)S(1)} %get-tuple-element.126), channel_id=1, replica_groups=mesh['row'=4,'col'=32] {'row','col'}, use_global_device_ids=true, to_apply=%region_10.11 | all-reduce | flops 256 | bytes 2048 | tf_op jit(solution)/shard_map/psum | solution.py:56
  516.7 1.7 broadcast_multiply_fusion
  518.3 116.3 %reduce-scatter.5.cloned.1.call-done = bf16[512,256]{1,0:T(8,128)(2,1)} async-done(((bf16[16384,256]{1,0:T(8,128)(2,1)}), bf16[512,256]{1,0:T(8,128)(2,1)}) %reduce-scatter.5.cloned.1.call-update) | async-done | bytes 262160 | tf_op jit(solution)/shard_map/reduce_scatter | solution.py:70
  (61 shorter events, 7.3 us)
Async XLA Ops:
  7.2 249.1 %copy-start = (bf16[256,256]{1,0:T(8,128)(2,1)S(1)}, bf16[256,256]{1,0:T(8,128)(2,1)}, u32[]{:S(2)}) copy-start(bf16[256,256]{1,0:T(8,128)(2,1)} %param.15) | copy-start | bytes 393220
  7.2 110.6 %all-gather.3.cloned.1.call-start = ((), (), s32[]{:S(2)}) async-start(), calls=%async_computation.2 | async-start | bytes 8650752 | tf_op jit(solution)/shard_map/all_gather | solution.py:27
  7.9 248.3 %reduce-scatter.3.cloned.1.call-start = ((), (), s32[]{:S(2)}) async-start(), calls=%async_computation.3 | async-start | bytes 1310720 | tf_op jit(solution)/shard_map/reduce_scatter | solution.py:52
  118.0 138.3 %copy-start.2 = (f32[256]{0:T(256)S(1)}, f32[256]{0:T(256)}, u32[]{:S(2)}) copy-start(f32[256]{0:T(256)} %param.16) | copy-start | bytes 3076
  179.5 101.9 %all-gather.5.cloned.1.call-start = ((), (), s32[]{:S(2)}) async-start(), calls=%async_computation.4 | async-start | bytes 1310720 | tf_op jit(solution)/shard_map/all_gather | solution.py:57
  259.4 257.3 %all-reduce.2.cloned.1.call-start = ((), (), s32[]{:S(2)}) async-start(), calls=%async_computation.6 | async-start | bytes 524288 | tf_op jit(solution)/shard_map/psum | solution.py:56
  261.4 373.2 %reduce-scatter.5.cloned.1.call-start = ((), (), s32[]{:S(2)}) async-start(), calls=%async_computation.5 | async-start | bytes 8650752 | tf_op jit(solution)/shard_map/reduce_scatter | solution.py:70
  281.4 7.8 %copy-start.1 = (bf16[2048,256]{1,0:T(8,128)(2,1)S(1)}, bf16[2048,256]{1,0:T(8,128)(2,1)}, u32[]{:S(2)}) copy-start(bf16[2048,256]{1,0:T(8,128)(2,1)} %all-gather.5.cloned.1.call-done) | copy-start | bytes 3145732
  281.4 7.8 %copy-start.3 = (s32[8]{0:T(128)S(1)}, s32[8]{0:T(128)}, u32[]{:S(2)}) copy-start(s32[8]{0:T(128)} %get-tuple-element.303) | copy-start | bytes 100
Sparse Core Ops, SparseCore 0:
  11.0 106.7 all-gather.2
  179.7 76.5 reduce-scatter.2
  259.5 21.8 all-gather.4
  287.3 142.8 all-reduce.1
  433.1 201.3 reduce-scatter.4
where the time goes:
time: 644 us; the launch traced here: 641 us
  waiting for transfers between devices  321 us (50%)
  blocking collectives  162 us (25%)
  other arithmetic  54.1 us (8%)
  local copies, waits for them, and re-layouts  40.7 us (6%)
  matrix products  36.5 us (6%)
  between operations  13.8 us (2%)
  loops' own time  12.1 us (2%)
    psum x1, blocking collectives, per_device(): weight_grad, bias_grad = lax.psum((weight_grad, bias_grad), ('row', 'col'))  162 us
    reduce_scatter x1, waiting for transfers between devices, per_device(): lax.psum_scatter(summed.astype(jnp.bfloat16), 'col', scatter_dimension=0,...  116 us
    all_gather x1, waiting for transfers between devices, per_device(): column_block = lax.all_gather(features, 'col', axis=0, tiled=True)  108 us
    reduce_scatter x1, waiting for transfers between devices, per_device(): lax.psum_scatter(partial_value.astype(jnp.bfloat16), 'row', scatter_dimen...  76.7 us
    scatter-add x8, other arithmetic, backward_slot(): return running.at[columns].add(contrib)  34.9 us
    gather x8, local copies, waits for them, and re-layouts, forward_slot(): jnp.take(x_tiles, columns, axis=0)  32 us
    all_gather x1, waiting for transfers between devices, per_device(): grad_block = lax.all_gather(hidden_grad, 'row', axis=0, tiled=True)  20 us
    dot_general x8, matrix products, forward_slot(): jnp.einsum('tij,tjf->tif', values, picked, preferred_element_type=jnp.flo...  17 us
  transfers between devices with their start and end apart: 5, of which 4 were waited for; matrix products, arithmetic and copies ran while one was open for 11% of the time, Pallas kernels for 0%

commit v1 on v0

--- a/solution.py
+++ b/solution.py
@@ -53,7 +53,7 @@
         partial_value.astype(jnp.bfloat16), "row", scatter_dimension=0, tiled=True
     )
     layer_out, weight_grad, bias_grad, hidden_grad = dense_part(own_rows, weight, bias, cotangent)
-    weight_grad, bias_grad = lax.psum((weight_grad, bias_grad), ("row", "col"))
+    weight_grad, bias_grad = lax.psum(lax.psum((weight_grad, bias_grad), "col"), "row")
     grad_block = lax.all_gather(hidden_grad, "row", axis=0, tiled=True)
     grad_tiles = grad_block.reshape(row_tiles, tile_size, width)
 

time: 644 us -> 972 us (1.51)
  waiting for transfers between devices: 321 us -> 666 us
  blocking collectives: 162 us -> 147 us
    psum x1 -> x2, waiting for transfers between devices: 0.01 us -> 348 us  [the longest x1 348 us: per_device(): lax.psum((weight_grad, bias_grad), 'col')]
    psum x1 -> x2, blocking collectives: 162 us -> 147 us  [the longest x1 138 us: per_device(): lax.psum((weight_grad, bias_grad), 'col')]
  transfers between devices with their start and end apart: 5 -> 6, of which waited for: 4 -> 5; matrix products, arithmetic and copies ran while one was open for 11% -> 7% of each run, Pallas kernels for 0% -> 0%
where the time goes in v1:
time: 972 us; the launch traced here: 969 us
  waiting for transfers between devices  666 us (69%)
  blocking collectives  147 us (15%)
  other arithmetic  54 us (6%)
  local copies, waits for them, and re-layouts  40.7 us (4%)
  matrix products  36.5 us (4%)
  between operations  14.2 us (1%)
  loops' own time  10.8 us (1%)
    psum x1, waiting for transfers between devices, per_device(): lax.psum((weight_grad, bias_grad), 'col')  348 us
    psum x1, blocking collectives, per_device(): lax.psum((weight_grad, bias_grad), 'col')  138 us
    reduce_scatter x1, waiting for transfers between devices, per_device(): lax.psum_scatter(summed.astype(jnp.bfloat16), 'col', scatter_dimension=0,...  110 us
    all_gather x1, waiting for transfers between devices, per_device(): column_block = lax.all_gather(features, 'col', axis=0, tiled=True)  108 us
    reduce_scatter x1, waiting for transfers between devices, per_device(): lax.psum_scatter(partial_value.astype(jnp.bfloat16), 'row', scatter_dimen...  76.1 us
    scatter-add x8, other arithmetic, backward_slot(): return running.at[columns].add(contrib)  34.8 us
    gather x8, local copies, waits for them, and re-layouts, forward_slot(): jnp.take(x_tiles, columns, axis=0)  32 us
    all_gather x1, waiting for transfers between devices, per_device(): grad_block = lax.all_gather(hidden_grad, 'row', axis=0, tiled=True)  23.2 us
  transfers between devices with their start and end apart: 6, of which 5 were waited for; matrix products, arithmetic and copies ran while one was open for 7% of the time, Pallas kernels for 0%

profile of v1, /device:TPU:0, one launch (start us, length us, event | category | flops | bytes accessed | tf_op | source)
XLA Modules:
  0.0 969.5 jit_solution(18244868971362568857)
XLA Ops:
  8.7 1.3 reduce_max.9
  10.0 107.8 %all-gather.3.cloned.1.call-done = bf16[16384,256]{1,0:T(8,128)(2,1)} async-done(((bf16[512,256]{1,0:T(8,128)(2,1)}), bf16[16384,256]{1,0:T(8,128)(2,1)}) %all-gather.3.cloned.1.call-update) | async-done | bytes 8388624 | tf_op jit(solution)/shard_map/all_gather | solution.py:27
  118.0 59.8 %while.20 = (s32[]{:T(128)}, f32[8,256,256]{2,1,0:T(8,128)S(1)}, s32[]{:T(128)}, bf16[8,16,256,256]{3,2,1,0:T(8,128)(2,1)}, s32[8,16]{0,1:T(8,128)S(1)}, /*index...) while((s32[]{:T(128)}, f32[8,256,256]{2,1,0:T(8,128)S(1)}, s32[]{:T(128)}, ...), condition=%wide.region_2.3_spmd, body=%wide.region_1.2_spmd.sunk | while | flops 270009408 | bytes 8393067 | solution.py:46
  119.2 4.0 gather_fusion
  123.2 2.1 convolution_add_fusion.3
  126.6 4.0 gather_fusion
  130.6 2.1 convolution_add_fusion.3
  134.0 4.0 gather_fusion
  138.0 2.1 convolution_add_fusion.3
  141.4 4.0 gather_fusion
  145.4 2.1 convolution_add_fusion.3
  148.8 4.0 gather_fusion
  152.9 2.1 convolution_add_fusion.3
  156.3 4.0 gather_fusion
  160.3 2.1 convolution_add_fusion.3
  163.7 4.0 gather_fusion
  167.7 2.1 convolution_add_fusion.3
  171.1 4.0 gather_fusion
  175.1 2.1 convolution_add_fusion.3
  177.8 1.1 convert_element_type.43
  178.9 76.1 %reduce-scatter.3.cloned.1.call-done = bf16[512,256]{1,0:T(8,128)(2,1)} async-done(((bf16[2048,256]{1,0:T(8,128)(2,1)}), bf16[512,256]{1,0:T(8,128)(2,1)}) %reduce-scatter.3.cloned.1.call-update) | async-done | bytes 262160 | tf_op jit(solution)/shard_map/reduce_scatter | solution.py:52
  255.1 2.1 convert_reduce_fusion
  257.2 1.9 fusion.13
  260.3 348.1 %all-reduce.3.cloned.1.call-done = f32[256,256]{1,0:T(8,128)} async-done(((f32[256,256]{1,0:T(8,128)}), f32[256,256]{1,0:T(8,128)}) %all-reduce.3.cloned.1.call-update) | async-done | bytes 262160 | tf_op jit(solution)/shard_map/psum | solution.py:56
  608.4 23.2 %all-gather.5.cloned.1.call-done = bf16[2048,256]{1,0:T(8,128)(2,1)} async-done(((bf16[512,256]{1,0:T(8,128)(2,1)}), bf16[2048,256]{1,0:T(8,128)(2,1)}) %all-gather.5.cloned.1.call-update) | async-done | bytes 1048592 | tf_op jit(solution)/shard_map/all_gather | solution.py:57
  631.7 7.8 broadcast_in_dim.21
  639.4 54.8 %while.21 = (s32[]{:T(128)}, f32[64,256,256]{2,1,0:T(8,128)}, s32[]{:T(128)}, s32[8,16]{0,1:T(8,128)S(1)}, bf16[8,16,256,256]{3,2,1,0:T(8,128)(2,1)}, /*index=5*...) while((s32[]{:T(128)}, f32[64,256,256]{2,1,0:T(8,128)}, s32[]{:T(128)}, ...), condition=%wide.region_6.7_spmd, body=%wide.region_4.6_spmd.sunk | while | flops 269484064 | bytes 10486107 | solution.py:66
  640.1 1.8 convolution_multiply_fusion.2
  641.9 4.3 scatter_fusion
  646.8 1.8 convolution_multiply_fusion.2
  648.6 4.4 scatter_fusion
  653.6 1.8 convolution_multiply_fusion.2
  655.4 4.2 scatter_fusion
  660.3 1.8 convolution_multiply_fusion.2
  662.1 4.4 scatter_fusion
  667.1 1.8 convolution_multiply_fusion.2
  668.9 4.4 scatter_fusion
  673.9 1.8 convolution_multiply_fusion.2
  675.7 4.4 scatter_fusion
  680.7 1.8 convolution_multiply_fusion.2
  682.5 4.4 scatter_fusion
  687.5 1.8 convolution_multiply_fusion.2
  689.3 4.3 scatter_fusion
  694.2 9.0 convert_element_type.49
  703.2 137.8 %psum.30 = f32[256]{0:T(256)S(1)} all-reduce(f32[256]{0:T(256)S(1)} %get-tuple-element.126), channel_id=1, replica_groups=mesh['row'=4,'col'=32] {'col'}, use_global_device_ids=true, to_apply=%region_11.12 | all-reduce | flops 256 | bytes 2048 | tf_op jit(solution)/shard_map/psum | solution.py:56
  841.0 9.6 psum.31
  851.2 1.7 broadcast_multiply_fusion
  852.8 109.8 %reduce-scatter.5.cloned.1.call-done = bf16[512,256]{1,0:T(8,128)(2,1)} async-done(((bf16[16384,256]{1,0:T(8,128)(2,1)}), bf16[512,256]{1,0:T(8,128)(2,1)}) %reduce-scatter.5.cloned.1.call-update) | async-done | bytes 262160 | tf_op jit(solution)/shard_map/reduce_scatter | solution.py:70
  (65 shorter events, 9.1 us)
Async XLA Ops:
  7.2 247.9 %copy-start = (bf16[256,256]{1,0:T(8,128)(2,1)S(1)}, bf16[256,256]{1,0:T(8,128)(2,1)}, u32[]{:S(2)}) copy-start(bf16[256,256]{1,0:T(8,128)(2,1)} %param.15) | copy-start | bytes 393220
  7.2 110.6 %all-gather.3.cloned.1.call-start = ((), (), s32[]{:S(2)}) async-start(), calls=%async_computation.2 | async-start | bytes 8650752 | tf_op jit(solution)/shard_map/all_gather | solution.py:27
  7.9 247.2 %reduce-scatter.3.cloned.1.call-start = ((), (), s32[]{:S(2)}) async-start(), calls=%async_computation.3 | async-start | bytes 1310720 | tf_op jit(solution)/shard_map/reduce_scatter | solution.py:52
  118.0 137.1 %copy-start.2 = (f32[256]{0:T(256)S(1)}, f32[256]{0:T(256)}, u32[]{:S(2)}) copy-start(f32[256]{0:T(256)} %param.16) | copy-start | bytes 3076
  178.9 429.5 %all-reduce.3.cloned.1.call-start = ((), (), s32[]{:S(2)}) async-start(), calls=%async_computation.6 | async-start | bytes 524288 | tf_op jit(solution)/shard_map/psum | solution.py:56
  259.2 372.5 %all-gather.5.cloned.1.call-start = ((), (), s32[]{:S(2)}) async-start(), calls=%async_computation.4 | async-start | bytes 1310720 | tf_op jit(solution)/shard_map/all_gather | solution.py:57
  260.2 590.9 %all-reduce.5.cloned.1.call-start = ((), (), s32[]{:S(2)}) async-start(), calls=%async_computation.7 | async-start | bytes 524288 | tf_op jit(solution)/shard_map/psum | solution.py:56
  608.4 354.2 %reduce-scatter.5.cloned.1.call-start = ((), (), s32[]{:S(2)}) async-start(), calls=%async_computation.5 | async-start | bytes 8650752 | tf_op jit(solution)/shard_map/reduce_scatter | solution.py:70
  631.7 7.8 copy-start.1
  631.7 7.8 copy-start.3
Sparse Core Ops, SparseCore 0:
  11.0 106.7 all-gather.2
  179.0 76.0 reduce-scatter.2
  259.3 349.0 all-reduce.2
  610.5 21.1 all-gather.4
  634.0 36.9 all-reduce.4
  703.3 259.2 reduce-scatter.4
